TPU v7x, 32 devices: a whole 2x2x4 slice. The times are simulated.
32 devices in a mesh: ctx: 8 (over z, core), fsdp: 4 (over y, x).
Axes of the slice: x: 2, y: 2, z: 4, core: 2. Of those that a mesh axis runs over, the one named last changes fastest.
Arguments:
- tokens: bfloat16 [4, 1024, 2048], P('fsdp', 'ctx'), may hold values from -6 to 6
- cotangent: bfloat16 [4, 1024, 2048], P('fsdp', 'ctx'), may hold values from -6 to 6
- doc_ids: int32 [4, 1024], P('fsdp'), may hold values from 0 to 3, never falling along the last dimension, each value on 1 to 512 neighbouring positions
- block_order: int32 [16], replicated, may hold values from 0 to 15, each once
- front_weight: bfloat16 [2048, 14336], P(None, 'fsdp'), may hold values from -0.125 to 0.125
- back_weight: bfloat16 [10240, 2048], P(None, 'fsdp'), may hold values from -2 to 2
- front_master: float32 [2048, 14336], P('ctx', 'fsdp'), may hold values from -0.125 to 0.125
- back_master: float32 [10240, 2048], P('ctx', 'fsdp'), may hold values from -0.0625 to 0.0625
- front_first: float32 [2048, 14336], P('ctx', 'fsdp'), may hold values from -64 to 64
- back_first: float32 [10240, 2048], P('ctx', 'fsdp'), may hold values from -64 to 64
- front_second: float32 [2048, 14336], P('ctx', 'fsdp'), may hold values from 100 to 10000
- back_second: float32 [10240, 2048], P('ctx', 'fsdp'), may hold values from 2.048 to 204.8
- vectors: float32 [20480], replicated, may hold values from -2 to 2
- vector_first: float32 [20480], replicated, may hold values from -64 to 64
- vector_second: float32 [20480], replicated, may hold values from 100 to 10000
- learn_rates: float32 [3], replicated, may hold values from 0.02 to 0.2
- adam_step: int32 [1], replicated, may hold values from 1 to 8
Outputs:
- layer_out: bfloat16 [4, 1024, 2048], P('fsdp', 'ctx')
- tokens_grad: bfloat16 [4, 1024, 2048], P('fsdp', 'ctx')
- front_grad: float32 [2048, 14336], P('ctx', 'fsdp')
- back_grad: float32 [10240, 2048], P('ctx', 'fsdp')
- vector_grad: float32 [20480], replicated
- front_new: float32 [2048, 14336], P('ctx', 'fsdp')
- back_new: float32 [10240, 2048], P('ctx', 'fsdp')
- vectors_new: float32 [20480], replicated
- front_first_new: float32 [2048, 14336], P('ctx', 'fsdp')
- back_first_new: float32 [10240, 2048], P('ctx', 'fsdp')
- vector_first_new: float32 [20480], replicated
- front_second_new: float32 [2048, 14336], P('ctx', 'fsdp')
- back_second_new: float32 [10240, 2048], P('ctx', 'fsdp')
- vector_second_new: float32 [20480], replicated
- front_next: bfloat16 [2048, 14336], P(None, 'fsdp')
- back_next: bfloat16 [10240, 2048], P(None, 'fsdp')
Inputs may be any that keep to these rules, and one draw needn't show every extreme that they name: `doc_ids`: within a sequence document numbers never fall; a document has 1 to 512 tokens, and one has exactly 512. `block_order`: A permutation of the block numbers.
All inputs are finite; a program needn't handle non-finite values.
Results may differ from a plain program's by a relative error of at most 0.02.
Values may be sent and summed in bfloat16 or wider, within the bound.
A program may use at most 512 MiB of HBM per device.

v0:
```python
import jax
import jax.numpy as jnp
from jax import lax
from jax.sharding import PartitionSpec as P

D = 2048
HEADS = 32
ROT = 32
HEAD_DIM = 64
IN_COLS = 14336
norm_eps = 1e-05
beta_first = 0.9
beta_second = 0.95
adam_eps = 1e-08
weight_decay = 0.1
masked_score = -1e30


def key_block(amount):
    for candidate in (512, 256, 128):
        return candidate
    return amount


def rotary_tables(positions):
    half_rot = ROT // 2
    frequency = jnp.power(10000.0, -2.0 * jnp.arange(half_rot, dtype=jnp.float32) / ROT)
    angles = positions.astype(jnp.float32)[:, None] * frequency[None, :]
    return (jnp.cos(angles), jnp.sin(angles))


def rotate(values, cosine, sine):
    half_rot = ROT // 2
    lower_half = values[..., :half_rot]
    upper_half = values[..., half_rot:ROT]
    cos_full = cosine[:, None, :]
    sin_full = sine[:, None, :]
    return jnp.concatenate(
        [
            lower_half * cos_full - upper_half * sin_full,
            upper_half * cos_full + lower_half * sin_full,
            values[..., ROT:],
        ],
        axis=-1,
    )


def layer_norm(values, norm_gain, norm_shift):
    row_mean = jnp.mean(values, axis=-1, keepdims=True)
    centered = values - row_mean
    variance = jnp.mean(centered * centered, axis=-1, keepdims=True)
    return centered * lax.rsqrt(variance + norm_eps) * norm_gain + norm_shift


def gelu_tanh(values):
    return jax.nn.gelu(values, approximate=True)


def stored_layout(doc_row, block_order):
    block_count = block_order.shape[0]
    block_tokens = doc_row.shape[0] // block_count
    offsets = jnp.arange(block_tokens, dtype=jnp.int32)
    positions = (block_order[:, None] * block_tokens + offsets[None, :]).reshape(-1)
    segments = jnp.take(doc_row.reshape(block_count, block_tokens), block_order, axis=0).reshape(-1)
    return (positions, segments)


def adam_update(weight, first, second, grad, rate, count_now, decay):
    first_new = beta_first * first + (1.0 - beta_first) * grad
    second_new = beta_second * second + (1.0 - beta_second) * grad * grad
    steps_float = count_now.astype(jnp.float32)
    first_fix = 1.0 - jnp.power(beta_first, steps_float)
    second_fix = 1.0 - jnp.power(beta_second, steps_float)
    change = first_new / first_fix / (jnp.sqrt(second_new / second_fix) + adam_eps) + decay * weight
    return (weight - rate * change, first_new, second_new)


def per_device(
    tokens,
    cotangent,
    doc_ids,
    block_order,
    front_weight,
    back_weight,
    front_master,
    back_master,
    front_first,
    back_first,
    front_second,
    back_second,
    vectors,
    vector_first,
    vector_second,
    learn_rates,
    adam_step,
):
    local_rows = tokens.shape[1]
    score_scale = HEAD_DIM ** (-0.5)
    contract_last = (((1,), (1,)), ((), ()))
    contract_first = (((0,), (0,)), ((), ()))
    bias_front = vectors[:IN_COLS]
    bias_back = vectors[IN_COLS : IN_COLS + D]
    norm_gain = vectors[IN_COLS + D : IN_COLS + 2 * D]
    norm_shift = vectors[IN_COLS + 2 * D :]
    positions_all, segments_all = stored_layout(doc_ids[0], block_order)
    seq_len = positions_all.shape[0]
    first_row = lax.axis_index("ctx") * local_rows
    query_pos = lax.dynamic_slice_in_dim(positions_all, first_row, local_rows)
    query_seg = lax.dynamic_slice_in_dim(segments_all, first_row, local_rows)
    inputs = tokens[0].astype(jnp.float32)
    normed, norm_pull = jax.vjp(layer_norm, inputs, norm_gain, norm_shift)
    normed_low = normed.astype(jnp.bfloat16)
    hidden = (
        jnp.dot(
            normed_low,
            lax.all_gather(front_weight, "fsdp", axis=1, tiled=True),
            preferred_element_type=jnp.float32,
        )
        + bias_front
    )
    cosine, sine = rotary_tables(query_pos)

    def rotate_pair(query_raw, key_raw):
        return (rotate(query_raw, cosine, sine), rotate(key_raw, cosine, sine))

    shaped = (local_rows, HEADS, HEAD_DIM)
    (query_rot, key_rot), rotary_pull = jax.vjp(
        rotate_pair, hidden[:, :D].reshape(shaped), hidden[:, D : 2 * D].reshape(shaped)
    )
    query_low = query_rot.astype(jnp.bfloat16)
    key_low = key_rot.reshape(local_rows, D).astype(jnp.bfloat16)
    value_low = hidden[:, 2 * D : 3 * D].astype(jnp.bfloat16)
    hidden_up = hidden[:, 3 * D :]

    def allowed_pairs(offset, block_len):
        key_pos = lax.dynamic_slice_in_dim(positions_all, offset, block_len)
        key_seg = lax.dynamic_slice_in_dim(segments_all, offset, block_len)
        return (key_pos[None, :] <= query_pos[:, None]) & (key_seg[None, :] == query_seg[:, None])

    start_state = (
        jnp.full((HEADS, local_rows), masked_score, jnp.float32),
        jnp.zeros((HEADS, local_rows), jnp.float32),
        jnp.zeros((HEADS, local_rows, HEAD_DIM), jnp.float32),
    )
    running = start_state
    key_piece = lax.all_gather(key_low, "ctx", axis=0, tiled=True)
    value_piece = lax.all_gather(value_low, "ctx", axis=0, tiled=True)
    amount = key_piece.shape[0]
    block_len = key_block(amount)

    def absorb_one_block(carried, block_number):
        block_start = block_number * block_len
        key_part = lax.dynamic_slice_in_dim(key_piece, block_start, block_len).reshape(
            block_len, HEADS, HEAD_DIM
        )
        value_part = lax.dynamic_slice_in_dim(value_piece, block_start, block_len).reshape(
            block_len, HEADS, HEAD_DIM
        )
        allowed = allowed_pairs(block_start, block_len)
        running_max, running_sum, running_out = carried
        scores = (
            jnp.einsum("qhd,khd->hqk", query_low, key_part, preferred_element_type=jnp.float32)
            * score_scale
        )
        masked = jnp.where(allowed[None], scores, masked_score)
        new_max = jnp.maximum(running_max, jnp.max(masked, axis=-1))
        weights = jnp.where(allowed[None], jnp.exp(masked - new_max[..., None]), 0.0)
        factor = jnp.exp(running_max - new_max)
        running_sum = running_sum * factor + jnp.sum(weights, axis=-1)
        running_out = running_out * factor[..., None] + jnp.einsum(
            "hqk,khd->hqd",
            weights.astype(jnp.bfloat16),
            value_part,
            preferred_element_type=jnp.float32,
        )
        carried = (new_max, running_sum, running_out)
        return (carried, None)

    running, unused = lax.scan(absorb_one_block, running, jnp.arange(amount // block_len))
    final_max, final_sum, final_out = running
    attended = jnp.transpose(final_out / final_sum[..., None], (1, 0, 2))
    log_total = final_max + jnp.log(final_sum)
    attended_low = attended.reshape(local_rows, D).astype(jnp.bfloat16)
    activation, gelu_pull = jax.vjp(gelu_tanh, hidden_up)
    mixed_low = jnp.concatenate([attended_low, activation.astype(jnp.bfloat16)], axis=1)
    projected = jnp.dot(
        mixed_low,
        lax.all_gather(back_weight, "fsdp", axis=1, tiled=True),
        preferred_element_type=jnp.float32,
    )
    layer_out = (inputs + projected + bias_back).astype(jnp.bfloat16)[None]
    grad_low = cotangent[0]
    grad_cols = grad_low
    mixed_grad = lax.dot_general(
        grad_cols,
        lax.all_gather(back_weight, "fsdp", axis=1, tiled=True),
        contract_last,
        preferred_element_type=jnp.float32,
    )
    attended_grad = mixed_grad[:, :D].reshape(shaped).astype(jnp.bfloat16)
    (up_grad,) = gelu_pull(mixed_grad[:, D:])
    row_delta = jnp.sum(attended_grad.astype(jnp.float32) * attended, axis=-1).T
    back_state = (jnp.zeros(shaped, jnp.float32), jnp.zeros((seq_len, 2 * D), jnp.float32))
    running = back_state
    scatter_key_piece = lax.all_gather(key_low, "ctx", axis=0, tiled=True)
    scatter_value_piece = lax.all_gather(value_low, "ctx", axis=0, tiled=True)
    amount = scatter_key_piece.shape[0]
    scatter_block_len = key_block(amount)

    def scatter_one_block(carried, block_number):
        block_start = block_number * scatter_block_len
        key_part = lax.dynamic_slice_in_dim(
            scatter_key_piece, block_start, scatter_block_len
        ).reshape(scatter_block_len, HEADS, HEAD_DIM)
        value_part = lax.dynamic_slice_in_dim(
            scatter_value_piece, block_start, scatter_block_len
        ).reshape(scatter_block_len, HEADS, HEAD_DIM)
        allowed = allowed_pairs(block_start, scatter_block_len)
        query_grad, key_value_grad = carried
        scores = (
            jnp.einsum("qhd,khd->hqk", query_low, key_part, preferred_element_type=jnp.float32)
            * score_scale
        )
        probs = jnp.where(allowed[None], jnp.exp(scores - log_total[..., None]), 0.0)
        value_grad = jnp.einsum(
            "hqk,qhd->khd",
            probs.astype(jnp.bfloat16),
            attended_grad,
            preferred_element_type=jnp.float32,
        )
        prob_grad = jnp.einsum(
            "qhd,khd->hqk", attended_grad, value_part, preferred_element_type=jnp.float32
        )
        score_grad = (probs * (prob_grad - row_delta[..., None])).astype(jnp.bfloat16)
        query_grad = (
            query_grad
            + jnp.einsum("hqk,khd->qhd", score_grad, key_part, preferred_element_type=jnp.float32)
            * score_scale
        )
        key_grad = (
            jnp.einsum("hqk,qhd->khd", score_grad, query_low, preferred_element_type=jnp.float32)
            * score_scale
        )
        block_grads = jnp.concatenate(
            [key_grad.reshape(scatter_block_len, D), value_grad.reshape(scatter_block_len, D)],
            axis=1,
        )
        key_value_grad = lax.dynamic_update_slice_in_dim(
            key_value_grad, block_grads, block_start, 0
        )
        carried = (query_grad, key_value_grad)
        return (carried, None)

    running, unused = lax.scan(scatter_one_block, running, jnp.arange(amount // scatter_block_len))
    query_grad, key_value_all = running
    key_value_own = lax.psum_scatter(
        key_value_all.astype(jnp.bfloat16), "ctx", scatter_dimension=0, tiled=True
    ).astype(jnp.float32)
    query_pre, key_pre = rotary_pull((query_grad, key_value_own[:, :D].reshape(shaped)))
    hidden_grad = jnp.concatenate(
        [
            query_pre.reshape(local_rows, D),
            key_pre.reshape(local_rows, D),
            key_value_own[:, D:],
            up_grad,
        ],
        axis=1,
    ).astype(jnp.bfloat16)
    grad_cols = hidden_grad
    normed_grad = lax.dot_general(
        grad_cols,
        lax.all_gather(front_weight, "fsdp", axis=1, tiled=True),
        contract_last,
        preferred_element_type=jnp.float32,
    )
    input_grad, gain_grad, shift_grad = norm_pull(normed_grad)
    tokens_grad = (grad_low.astype(jnp.float32) + input_grad).astype(jnp.bfloat16)[None]
    front_term = lax.psum_scatter(
        lax.dot_general(
            normed_low, hidden_grad, contract_first, preferred_element_type=jnp.float32
        ).astype(jnp.bfloat16),
        "ctx",
        scatter_dimension=0,
        tiled=True,
    )
    back_term = lax.psum_scatter(
        lax.dot_general(
            mixed_low, grad_low, contract_first, preferred_element_type=jnp.float32
        ).astype(jnp.bfloat16),
        "ctx",
        scatter_dimension=0,
        tiled=True,
    )
    front_grad, back_grad = (
        lax.psum_scatter(front_term, "fsdp", scatter_dimension=1, tiled=True).astype(jnp.float32),
        lax.psum_scatter(back_term, "fsdp", scatter_dimension=1, tiled=True).astype(jnp.float32),
    )
    vector_term = jnp.concatenate(
        [
            jnp.sum(hidden_grad, axis=0, dtype=jnp.float32),
            jnp.sum(grad_low, axis=0, dtype=jnp.float32),
            gain_grad,
            shift_grad,
        ]
    )
    vector_grad = lax.psum(vector_term, ("ctx", "fsdp"))
    count_now = adam_step[0]
    front_new, front_first_new, front_second_new = adam_update(
        front_master, front_first, front_second, front_grad, learn_rates[0], count_now, weight_decay
    )
    back_new, back_first_new, back_second_new = adam_update(
        back_master, back_first, back_second, back_grad, learn_rates[1], count_now, weight_decay
    )
    vectors_new, vector_first_new, vector_second_new = adam_update(
        vectors, vector_first, vector_second, vector_grad, learn_rates[2], count_now, 0.0
    )
    front_next, back_next = (
        lax.all_gather(front_new.astype(jnp.bfloat16), "ctx", axis=0, tiled=True),
        lax.all_gather(back_new.astype(jnp.bfloat16), "ctx", axis=0, tiled=True),
    )
    return (
        layer_out,
        tokens_grad,
        front_grad,
        back_grad,
        vector_grad,
        front_new,
        back_new,
        vectors_new,
        front_first_new,
        back_first_new,
        vector_first_new,
        front_second_new,
        back_second_new,
        vector_second_new,
        front_next,
        back_next,
    )


def solution(mesh):
    in_specs = (
        P("fsdp", "ctx", None),
        P("fsdp", "ctx", None),
        P("fsdp", None),
        P(),
        P(None, "fsdp"),
        P(None, "fsdp"),
        P("ctx", "fsdp"),
        P("ctx", "fsdp"),
        P("ctx", "fsdp"),
        P("ctx", "fsdp"),
        P("ctx", "fsdp"),
        P("ctx", "fsdp"),
        P(),
        P(),
        P(),
        P(),
        P(),
    )
    out_specs = (
        P("fsdp", "ctx", None),
        P("fsdp", "ctx", None),
        P("ctx", "fsdp"),
        P("ctx", "fsdp"),
        P(),
        P("ctx", "fsdp"),
        P("ctx", "fsdp"),
        P(),
        P("ctx", "fsdp"),
        P("ctx", "fsdp"),
        P(),
        P("ctx", "fsdp"),
        P("ctx", "fsdp"),
        P(),
        P(None, "fsdp"),
        P(None, "fsdp"),
    )
    return jax.shard_map(
        per_device, mesh=mesh, in_specs=in_specs, out_specs=out_specs, check_vma=False
    )
```

profile of v0, /device:TPU:0, one launch (start us, length us, event | category | flops | bytes accessed | tf_op | source)
XLA Modules:
  0.0 2660.3 jit_solution(6433679246068548918)
XLA Ops:
  10.5 509.2 %all-gather.7.cloned.1.call-done = bf16[2048,14336]{1,0:T(8,128)(2,1)} async-done(((bf16[2048,3584]{1,0:T(8,128)(2,1)}), bf16[2048,14336]{1,0:T(8,128)(2,1)}) %all-gather.7.cloned.1.call-update) | async-done | bytes 58720272 | tf_op jit(solution)/shard_map/all_gather | solution.py:116
  519.8 31.0 %convolution_add_fusion = f32[128,14336]{1,0:T(8,128)} fusion(bf16[2048,14336]{1,0:T(8,128)(2,1)} %all-gather.7.cloned.1.call-done, f32[14336]{0:T(1024)S(1)} %slice-done, bf16[1,128,2048]{2,1,0:T(8,128)(2,1)S(1)} %copy-done, f32[2048]{0:T(1024)S(1)} %get-tuple-element.415, f32[2048]{0:T(1024)S(1)} %get-tuple-element.416, f32[128]{0:T(128)S(1)} %fusion.56, ...), kind=kOutput, calls=%fused_computation.42 | convolution fusion | flops 7519600640 | bytes 66659328 | tf_op jit(solution)/shard_map/dot_general | solution.py:114
  561.5 327.4 %all-gather.13.cloned.1.call-done = bf16[10240,2048]{1,0:T(8,128)(2,1)} async-done(((bf16[10240,512]{1,0:T(8,128)(2,1)}), bf16[10240,2048]{1,0:T(8,128)(2,1)}) %all-gather.13.cloned.1.call-update) | async-done | bytes 41943056 | tf_op jit(solution)/shard_map/all_gather | solution.py:188
  888.9 21.6 fusion.53
  913.2 24.8 all-gather.11.cloned.1.call-done
  944.4 42.2 %all-gather.9.cloned.1.call-done = bf16[1024,2048]{0,1:T(8,128)(2,1)} async-done(((bf16[128,2048]{0,1:T(8,128)(2,1)}), bf16[1024,2048]{0,1:T(8,128)(2,1)}) %all-gather.9.cloned.1.call-update) | async-done | bytes 4194320 | tf_op jit(solution)/shard_map/all_gather | solution.py:146
  986.7 22.1 while.28
  1013.5 54.8 %while.29 = (s32[]{:T(128)}, f32[128,32,64]{0,2,1:T(8,128)S(1)}, bf16[1024,4096]{1,0:T(8,128)(2,1)}, s32[2]{0:T(128)S(1)}, bf16[1024,2048]{0,1:T(8,128)(2,1)}, /...) while((s32[]{:T(128)}, f32[128,32,64]{0,2,1:T(8,128)S(1)}, ...), condition=%wide.region_8.9_spmd.clone, body=%wide.region_7.8_spmd.clone.sunk | while | flops 1374617600 | bytes 86242552 | solution.py:254
  1068.3 6.7 fusion.31
  1077.2 18.6 convolution_convert_fusion.1
  1096.0 60.2 %reduce-scatter.8.cloned.1.call-done = bf16[128,4096]{1,0:T(8,128)(2,1)} async-done(((bf16[1024,4096]{1,0:T(8,128)(2,1)}), bf16[128,4096]{1,0:T(8,128)(2,1)}) %reduce-scatter.8.cloned.1.call-update) | async-done | bytes 1048592 | tf_op jit(solution)/shard_map/reduce_scatter | solution.py:256
  1164.4 24.0 convolution_convert_fusion
  1188.5 372.6 %reduce-scatter.16.cloned.1.call-done = bf16[1280,2048]{1,0:T(8,128)(2,1)} async-done(((bf16[10240,2048]{1,0:T(8,128)(2,1)}), bf16[1280,2048]{1,0:T(8,128)(2,1)}) %reduce-scatter.16.cloned.1.call-update) | async-done | bytes 5242896
  1561.2 562.6 %reduce-scatter.10.cloned.1.call-done = bf16[256,14336]{1,0:T(8,128)(2,1)} async-done(((bf16[2048,14336]{1,0:T(8,128)(2,1)}), bf16[256,14336]{1,0:T(8,128)(2,1)}) %reduce-scatter.10.cloned.1.call-update) | async-done | bytes 7340048 | tf_op jit(solution)/shard_map/reduce_scatter | solution.py:278
  2125.3 27.8 %fusion.48 = (f32[128]{0:T(128)S(1)}, f32[128,2048]{1,0:T(8,128)}) fusion(bf16[1,128,2048]{2,1,0:T(8,128)(2,1)S(1)} %copy-done.1, f32[2048]{0:T(1024)S(1)} %copy-done.14, f32[128]{0:T(128)S(1)} %copy-done.20, bf16[2048,14336]{1,0:T(8,128)(2,1)} %all-gather.7.cloned.1.call-done, bf16[128,8192]{1,0:T(8,128)(2,1)S(1)} %copy-done.3, ...), kind=kOutput, calls=%fused_computation.84 | convolution fusion | flops 7532183552 | bytes 63972352 | tf_op jit(solution)/shard_map/dot_general | solution.py:270
  2159.1 27.5 %reduce-scatter.14.cloned.1.call-done = bf16[1280,512]{1,0:T(8,128)(2,1)} async-done(((bf16[1280,2048]{1,0:T(8,128)(2,1)}), bf16[1280,512]{1,0:T(8,128)(2,1)}) %reduce-scatter.14.cloned.1.call-update) | async-done | bytes 1310736 | tf_op jit(solution)/shard_map/reduce_scatter | solution.py:296
  2186.6 8.3 fusion.63
  2195.0 73.3 %reduce-scatter.12.cloned.1.call-done = bf16[256,3584]{1,0:T(8,128)(2,1)} async-done(((bf16[256,14336]{1,0:T(8,128)(2,1)}), bf16[256,3584]{1,0:T(8,128)(2,1)}) %reduce-scatter.12.cloned.1.call-update) | async-done | bytes 1835024 | tf_op jit(solution)/shard_map/reduce_scatter | solution.py:295
  2268.4 10.9 fusion.65
  2279.3 16.8 fusion.36
  2296.1 99.7 %all-reduce.9.cloned.1.call-done = f32[20480]{0:T(1024)} async-done(((f32[20480]{0:T(1024)}), f32[20480]{0:T(1024)}) %all-reduce.9.cloned.1.call-update) | async-done | bytes 81936 | tf_op jit(solution)/shard_map/psum | solution.py:306
  2398.1 101.5 %all-gather.17.cloned.1.call-done = bf16[10240,512]{1,0:T(8,128)(2,1)} async-done(((bf16[1280,512]{1,0:T(8,128)(2,1)}), bf16[10240,512]{1,0:T(8,128)(2,1)}) %all-gather.17.cloned.1.call-update) | async-done | bytes 10485776 | tf_op jit(solution)/shard_map/all_gather | solution.py:319
  2499.6 134.3 %all-gather.15.cloned.1.call-done = bf16[2048,3584]{1,0:T(8,128)(2,1)} async-done(((bf16[256,3584]{1,0:T(8,128)(2,1)}), bf16[2048,3584]{1,0:T(8,128)(2,1)}) %all-gather.15.cloned.1.call-update) | async-done | bytes 14680080 | tf_op jit(solution)/shard_map/all_gather | solution.py:318
  2635.4 13.7 copy.134
  (205 shorter events, 126.5 us)
Async XLA Ops:
  7.2 512.6 %all-gather.7.cloned.1.call-start = ((), (), s32[]{:S(2)}) async-start(), calls=%async_computation.5 | async-start | bytes 73400320 | tf_op jit(solution)/shard_map/all_gather | solution.py:116
  7.9 511.8 %slice-start = ((f32[20480]{0:T(1024)}), f32[14336]{0:T(1024)S(1)}, s32[]{:S(2)}) async-start(f32[20480]{0:T(1024)} %param.33), calls=%async_computation.17 | async-start | bytes 114688 | tf_op jit(solution)/shard_map/slice | solution.py:101
  7.9 881.0 %all-gather.13.cloned.1.call-start = ((), (), s32[]{:S(2)}) async-start(), calls=%async_computation.8 | async-start | bytes 52428800 | tf_op jit(solution)/shard_map/all_gather | solution.py:188
  8.7 929.3 %all-gather.11.cloned.1.call-start = ((), (), s32[]{:S(2)}) async-start(), calls=%async_computation.7 | async-start | bytes 4718592 | tf_op jit(solution)/shard_map/all_gather | solution.py:147
  9.1 541.7 %copy-start.19 = (f32[128]{0:T(128)}, f32[128]{0:T(128)S(1)}, u32[]{:S(2)}) copy-start(f32[128]{0:T(128)S(1)} %broadcast_multiply_fusion) | copy-start | bytes 1540
  9.9 540.9 %copy-start.21 = (f32[128]{0:T(128)}, f32[128]{0:T(128)S(1)}, u32[]{:S(2)}) copy-start(f32[128]{0:T(128)S(1)} %fusion.56) | copy-start | bytes 1540
  10.5 540.2 %copy-start.13 = (f32[2048]{0:T(1024)}, f32[2048]{0:T(1024)S(1)}, u32[]{:S(2)}) copy-start(f32[2048]{0:T(1024)S(1)} %get-tuple-element.416) | copy-start | bytes 24580
  10.5 540.3 %copy-start.15 = (f32[2048]{0:T(1024)}, f32[2048]{0:T(1024)S(1)}, u32[]{:S(2)}) copy-start(f32[2048]{0:T(1024)S(1)} %get-tuple-element.415) | copy-start | bytes 24580
  553.0 433.7 %all-gather.9.cloned.1.call-start = ((), (), s32[]{:S(2)}) async-start(), calls=%async_computation.6 | async-start | bytes 4718592 | tf_op jit(solution)/shard_map/all_gather | solution.py:146
  555.2 333.7 %copy-start.5 = (bf16[1,128,2048]{2,1,0:T(8,128)(2,1)S(1)}, bf16[1,128,2048]{2,1,0:T(8,128)(2,1)}, u32[]{:S(2)}) copy-start(bf16[1,128,2048]{2,1,0:T(8,128)(2,1)} %param.22) | copy-start | bytes 1572868
  559.0 597.1 %reduce-scatter.8.cloned.1.call-start = ((), (), s32[]{:S(2)}) async-start(), calls=%async_computation.9 | async-start | bytes 9437184 | tf_op jit(solution)/shard_map/reduce_scatter | solution.py:256
  1068.3 492.8 %reduce-scatter.16.cloned.1.call-start = ((), (), s32[]{:S(2)}) async-start(), calls=%async_computation.16 | async-start | bytes 47185920
  1095.8 66.5 %copy-start.26 = (f32[128,16]{0,1:T(8,128)S(1)}, f32[128,16]{0,1:T(8,128)}, u32[]{:S(2)}) copy-start(f32[128,16]{0,1:T(8,128)} %copy-done.25) | copy-start | bytes 24580
  1095.9 1027.9 %reduce-scatter.10.cloned.1.call-start = ((), (), s32[]{:S(2)}) async-start(), calls=%async_computation.10 | async-start | bytes 66060288 | tf_op jit(solution)/shard_map/reduce_scatter | solution.py:278
  1188.5 998.2 %reduce-scatter.14.cloned.1.call-start = ((), (), s32[]{:S(2)}) async-start(), calls=%async_computation.12 | async-start | bytes 6553600 | tf_op jit(solution)/shard_map/reduce_scatter | solution.py:296
  1561.2 563.4 %copy-start.30 = (f32[3]{0:T(128)S(1)}, f32[3]{0:T(128)}, u32[]{:S(2)}) copy-start(f32[3]{0:T(128)} %param.36) | copy-start | bytes 40
  1561.2 564.1 %copy-start.3 = (bf16[128,8192]{1,0:T(8,128)(2,1)S(1)}, bf16[128,8192]{1,0:T(8,128)(2,1)}, u32[]{:S(2)}) copy-start(bf16[128,8192]{1,0:T(8,128)(2,1)} %get-tuple-element.398) | copy-start | bytes 6291460
  1561.2 707.2 %reduce-scatter.12.cloned.1.call-start = ((), (), s32[]{:S(2)}) async-start(), calls=%async_computation.11 | async-start | bytes 9175040 | tf_op jit(solution)/shard_map/reduce_scatter | solution.py:295
  2123.8 272.0 %all-reduce.9.cloned.1.call-start = ((), (), s32[]{:S(2)}) async-start(), calls=%async_computation.13 | async-start | bytes 163840 | tf_op jit(solution)/shard_map/psum | solution.py:306
  2159.1 340.5 %all-gather.17.cloned.1.call-start = ((), (), s32[]{:S(2)}) async-start(), calls=%async_computation.15 | async-start | bytes 11796480 | tf_op jit(solution)/shard_map/all_gather | solution.py:319
  2195.0 438.9 %all-gather.15.cloned.1.call-start = ((), (), s32[]{:S(2)}) async-start(), calls=%async_computation.14 | async-start | bytes 16515072 | tf_op jit(solution)/shard_map/all_gather | solution.py:318
  2279.3 116.5 %copy-start.18 = (f32[20480]{0:T(1024)S(1)}, f32[20480]{0:T(1024)}, u32[]{:S(2)}) copy-start(f32[20480]{0:T(1024)} %param.33) | copy-start | bytes 245764
  2279.3 116.5 %copy-start.23 = (f32[20480]{0:T(1024)S(1)}, f32[20480]{0:T(1024)}, u32[]{:S(2)}) copy-start(f32[20480]{0:T(1024)} %param.35) | copy-start | bytes 245764
  2279.3 116.5 %copy-start.24 = (f32[20480]{0:T(1024)S(1)}, f32[20480]{0:T(1024)}, u32[]{:S(2)}) copy-start(f32[20480]{0:T(1024)} %param.34) | copy-start | bytes 245764
  (24 other events, 271.8 us)
Sparse Core Ops, SparseCore 0:
  9.8 509.8 all-gather.6
  521.6 367.2 all-gather.12
  891.1 46.8 all-gather.10
  940.0 46.5 all-gather.8
  1068.4 87.6 reduce-scatter.7
  1158.4 402.7 reduce-scatter.15
  1563.5 560.2 reduce-scatter.9
  2126.8 59.8 reduce-scatter.13
  2189.6 78.7 reduce-scatter.11
  2274.4 121.3 all-reduce.8
  2398.1 101.4 all-gather.16
  2501.6 132.2 all-gather.14
where the time goes:
time: 2670 us; the launch traced here: 2660 us
  waiting for transfers between devices  2340 us (88%)
  matrix products  169 us (6%)
  local copies, waits for them, and re-layouts  82.6 us (3%)
  other arithmetic  52.3 us (2%)
    reduce_scatter x1, waiting for transfers between devices, per_device(): lax.psum_scatter(lax.dot_general(normed_low, hidden_grad, contract_first,...  563 us
    all_gather x1, waiting for transfers between devices, per_device(): lax.all_gather(front_weight, 'fsdp', axis=1, tiled=True)  509 us
    unnamed x13, waiting for transfers between devices  374 us
    all_gather x1, waiting for transfers between devices, per_device(): lax.all_gather(back_weight, 'fsdp', axis=1, tiled=True)  327 us
    all_gather x1, waiting for transfers between devices, per_device(): lax.all_gather(front_new.astype(jnp.bfloat16), 'ctx', axis=0, tiled=True)  134 us
    all_gather x1, waiting for transfers between devices, per_device(): lax.all_gather(back_new.astype(jnp.bfloat16), 'ctx', axis=0, tiled=True)  102 us
    psum x1, waiting for transfers between devices, per_device(): vector_grad = lax.psum(vector_term, ('ctx', 'fsdp'))  99.7 us
    reduce_scatter x1, waiting for transfers between devices, per_device(): lax.psum_scatter(front_term, 'fsdp', scatter_dimension=1, tiled=True)  73.3 us
  transfers between devices with their start and end apart: 12, of which 12 were waited for; matrix products, arithmetic and copies ran while one was open for 8% of the time, Pallas kernels for 0%

commit v1 on v0

--- a/solution.py
+++ b/solution.py
@@ -14,6 +14,11 @@
 adam_eps = 1e-08
 weight_decay = 0.1
 masked_score = -1e30
+compute_rounds_here = lambda content, x_local, ax_name: jnp.split(
+    lax.all_gather(jnp.concatenate([content, x_local], axis=1), ax_name, axis=0, tiled=True),
+    [content.shape[1]],
+    1,
+)
 
 
 def key_block(amount):
@@ -143,8 +148,7 @@
         jnp.zeros((HEADS, local_rows, HEAD_DIM), jnp.float32),
     )
     running = start_state
-    key_piece = lax.all_gather(key_low, "ctx", axis=0, tiled=True)
-    value_piece = lax.all_gather(value_low, "ctx", axis=0, tiled=True)
+    key_piece, value_piece = compute_rounds_here(key_low, value_low, "ctx")
     amount = key_piece.shape[0]
     block_len = key_block(amount)
 

time: 2670 us -> 2770 us (1.037)
  matrix products: 169 us -> 218 us
  local copies, waits for them, and re-layouts: 82.6 us -> 111 us
    all_gather x2 -> x3, waiting for transfers between devices: 67 us -> 83.6 us  [the longest x1 59 us: lax.all_gather(jnp.concatenate([content, x_local], axis=1), ax_name, axis...]
    unnamed x13 -> x14, waiting for transfers between devices: 374 us -> 372 us
  transfers between devices with their start and end apart: 12 -> 13, of which waited for: 12 -> 12; matrix products, arithmetic and copies ran while one was open for 8% -> 10% of each run, Pallas kernels for 0% -> 0%
where the time goes in v1:
time: 2770 us; the launch traced here: 2760 us
  waiting for transfers between devices  2350 us (85%)
  matrix products  218 us (8%)
  local copies, waits for them, and re-layouts  111 us (4%)
  other arithmetic  61.6 us (2%)
    reduce_scatter x1, waiting for transfers between devices, per_device(): lax.psum_scatter(lax.dot_general(normed_low, hidden_grad, contract_first,...  563 us
    all_gather x1, waiting for transfers between devices, per_device(): lax.all_gather(front_weight, 'fsdp', axis=1, tiled=True)  509 us
    unnamed x14, waiting for transfers between devices  372 us
    all_gather x1, waiting for transfers between devices, per_device(): lax.all_gather(back_weight, 'fsdp', axis=1, tiled=True)  326 us
    all_gather x1, waiting for transfers between devices, per_device(): lax.all_gather(front_new.astype(jnp.bfloat16), 'ctx', axis=0, tiled=True)  134 us
    all_gather x1, waiting for transfers between devices, per_device(): lax.all_gather(back_new.astype(jnp.bfloat16), 'ctx', axis=0, tiled=True)  101 us
    psum x1, waiting for transfers between devices, per_device(): vector_grad = lax.psum(vector_term, ('ctx', 'fsdp'))  99.4 us
    reduce_scatter x1, waiting for transfers between devices, per_device(): lax.psum_scatter(front_term, 'fsdp', scatter_dimension=1, tiled=True)  73.1 us
  transfers between devices with their start and end apart: 13, of which 12 were waited for; matrix products, arithmetic and copies ran while one was open for 10% of the time, Pallas kernels for 0%

profile of v1, /device:TPU:0, one launch (start us, length us, event | category | flops | bytes accessed | tf_op | source)
XLA Modules:
  0.0 2759.7 jit_solution(5935328656028672768)
XLA Ops:
  10.8 509.0 %all-gather.8.cloned.1.call-done = bf16[2048,14336]{1,0:T(8,128)(2,1)} async-done(((bf16[2048,3584]{1,0:T(8,128)(2,1)}), bf16[2048,14336]{1,0:T(8,128)(2,1)}) %all-gather.8.cloned.1.call-update) | async-done | bytes 58720272 | tf_op jit(solution)/shard_map/all_gather | solution.py:121
  519.8 30.9 %convolution_add_fusion = f32[128,14336]{1,0:T(8,128)} fusion(bf16[2048,14336]{1,0:T(8,128)(2,1)} %all-gather.8.cloned.1.call-done, f32[14336]{0:T(1024)S(1)} %slice-done, bf16[1,128,2048]{2,1,0:T(8,128)(2,1)S(1)} %copy-done.3, f32[2048]{0:T(1024)S(1)} %get-tuple-element.415, f32[2048]{0:T(1024)S(1)} %get-tuple-element.416, f32[128]{0:T(128)S(1)} %fusion.56, ...), kind=kOutput, calls=%fused_computation.42 | convolution fusion | flops 7519600640 | bytes 66659328 | tf_op jit(solution)/shard_map/dot_general | solution.py:119
  562.5 326.4 %all-gather.12.cloned.1.call-done = bf16[10240,2048]{1,0:T(8,128)(2,1)} async-done(((bf16[10240,512]{1,0:T(8,128)(2,1)}), bf16[10240,2048]{1,0:T(8,128)(2,1)}) %all-gather.12.cloned.1.call-update) | async-done | bytes 41943056 | tf_op jit(solution)/shard_map/all_gather | solution.py:192
  888.9 22.0 fusion.53
  914.2 59.0 %all-gather.10.cloned.1.call-done = bf16[1024,4096]{1,0:T(8,128)(2,1)} async-done(((bf16[128,4096]{1,0:T(8,128)(2,1)}), bf16[1024,4096]{1,0:T(8,128)(2,1)}) %all-gather.10.cloned.1.call-update) | async-done | bytes 8388624 | tf_op jit(solution)/shard_map/all_gather | solution.py:18
  979.3 63.2 %while.28 = (s32[]{:T(128)}, f32[32,128]{1,0:T(8,128)S(1)}, f32[32,128]{1,0:T(8,128)S(1)}, f32[32,128,64]{1,2,0:T(8,128)}, s32[2]{0:T(128)S(1)}, /*index=5*/s32[...) while((s32[]{:T(128)}, f32[32,128]{1,0:T(8,128)S(1)}, ...), condition=%wide.region_5.6_spmd.clone, body=%wide.region_2.0_spmd.clone.sunk | while | flops 565137408 | bytes 49296620 | solution.py:183
  1044.1 24.6 all-gather.16.cloned.1.call-done
  1073.1 94.5 %while.29 = (s32[]{:T(128)}, f32[128,32,64]{0,2,1:T(8,128)}, bf16[1024,4096]{1,0:T(8,128)(2,1)}, s32[2]{0:T(128)S(1)}, bf16[1024,2048]{0,1:T(8,128)(2,1)}, /*ind...) while((s32[]{:T(128)}, f32[128,32,64]{0,2,1:T(8,128)}, ...), condition=%wide.region_8.9_spmd.clone, body=%wide.region_7.8_spmd.clone.sunk | while | flops 1374617600 | bytes 123991352 | solution.py:258
  1086.7 9.0 fusion.134
  1133.7 9.0 fusion.134
  1176.5 16.9 convolution_convert_fusion.1
  1195.5 60.5 %reduce-scatter.8.cloned.1.call-done = bf16[128,4096]{1,0:T(8,128)(2,1)} async-done(((bf16[1024,4096]{1,0:T(8,128)(2,1)}), bf16[128,4096]{1,0:T(8,128)(2,1)}) %reduce-scatter.8.cloned.1.call-update) | async-done | bytes 1048592 | tf_op jit(solution)/shard_map/reduce_scatter | solution.py:260
  1267.1 24.1 convolution_convert_fusion
  1291.2 370.0 %reduce-scatter.16.cloned.1.call-done = bf16[1280,2048]{1,0:T(8,128)(2,1)} async-done(((bf16[10240,2048]{1,0:T(8,128)(2,1)}), bf16[1280,2048]{1,0:T(8,128)(2,1)}) %reduce-scatter.16.cloned.1.call-update) | async-done | bytes 5242896
  1661.3 562.6 %reduce-scatter.10.cloned.1.call-done = bf16[256,14336]{1,0:T(8,128)(2,1)} async-done(((bf16[2048,14336]{1,0:T(8,128)(2,1)}), bf16[256,14336]{1,0:T(8,128)(2,1)}) %reduce-scatter.10.cloned.1.call-update) | async-done | bytes 7340048 | tf_op jit(solution)/shard_map/reduce_scatter | solution.py:282
  2225.3 27.6 fusion.48
  2258.8 27.9 %reduce-scatter.14.cloned.1.call-done = bf16[1280,512]{1,0:T(8,128)(2,1)} async-done(((bf16[1280,2048]{1,0:T(8,128)(2,1)}), bf16[1280,512]{1,0:T(8,128)(2,1)}) %reduce-scatter.14.cloned.1.call-update) | async-done | bytes 1310736 | tf_op jit(solution)/shard_map/reduce_scatter | solution.py:300
  2295.1 73.1 %reduce-scatter.12.cloned.1.call-done = bf16[256,3584]{1,0:T(8,128)(2,1)} async-done(((bf16[256,14336]{1,0:T(8,128)(2,1)}), bf16[256,3584]{1,0:T(8,128)(2,1)}) %reduce-scatter.12.cloned.1.call-update) | async-done | bytes 1835024 | tf_op jit(solution)/shard_map/reduce_scatter | solution.py:299
  2368.3 10.7 fusion.65
  2379.1 17.4 fusion.36
  2396.5 99.4 %all-reduce.9.cloned.1.call-done = f32[20480]{0:T(1024)} async-done(((f32[20480]{0:T(1024)}), f32[20480]{0:T(1024)}) %all-reduce.9.cloned.1.call-update) | async-done | bytes 81936 | tf_op jit(solution)/shard_map/psum | solution.py:310
  2498.2 100.8 %all-gather.20.cloned.1.call-done = bf16[10240,512]{1,0:T(8,128)(2,1)} async-done(((bf16[1280,512]{1,0:T(8,128)(2,1)}), bf16[10240,512]{1,0:T(8,128)(2,1)}) %all-gather.20.cloned.1.call-update) | async-done | bytes 10485776 | tf_op jit(solution)/shard_map/all_gather | solution.py:323
  2598.9 134.5 %all-gather.18.cloned.1.call-done = bf16[2048,3584]{1,0:T(8,128)(2,1)} async-done(((bf16[256,3584]{1,0:T(8,128)(2,1)}), bf16[2048,3584]{1,0:T(8,128)(2,1)}) %all-gather.18.cloned.1.call-update) | async-done | bytes 14680080 | tf_op jit(solution)/shard_map/all_gather | solution.py:322
  2734.9 13.7 copy.148
  (224 shorter events, 212.1 us)
Async XLA Ops:
  7.2 512.6 %all-gather.8.cloned.1.call-start = ((), (), s32[]{:S(2)}) async-start(), calls=%async_computation.5 | async-start | bytes 73400320 | tf_op jit(solution)/shard_map/all_gather | solution.py:121
  7.9 511.8 %slice-start = ((f32[20480]{0:T(1024)}), f32[14336]{0:T(1024)S(1)}, s32[]{:S(2)}) async-start(f32[20480]{0:T(1024)} %param.33), calls=%async_computation.18 | async-start | bytes 114688 | tf_op jit(solution)/shard_map/slice | solution.py:106
  8.0 881.0 %all-gather.12.cloned.1.call-start = ((), (), s32[]{:S(2)}) async-start(), calls=%async_computation.7 | async-start | bytes 52428800 | tf_op jit(solution)/shard_map/all_gather | solution.py:192
  8.7 964.5 %all-gather.10.cloned.1.call-start = ((), (), s32[]{:S(2)}) async-start(), calls=%async_computation.6 | async-start | bytes 9437184 | tf_op jit(solution)/shard_map/all_gather | solution.py:18
  9.2 510.6 %copy-start.20 = (f32[128]{0:T(128)}, f32[128]{0:T(128)S(1)}, u32[]{:S(2)}) copy-start(f32[128]{0:T(128)S(1)} %broadcast_multiply_fusion) | copy-start | bytes 1540
  9.5 510.3 %copy-start.22 = (f32[128]{0:T(128)}, f32[128]{0:T(128)S(1)}, u32[]{:S(2)}) copy-start(f32[128]{0:T(128)S(1)} %fusion.56) | copy-start | bytes 1540
  10.1 546.6 %copy-start.26 = (f32[128,16]{0,1:T(8,128)}, f32[128,16]{0,1:T(8,128)S(1)}, u32[]{:S(2)}) copy-start(f32[128,16]{0,1:T(8,128)S(1)} %get-tuple-element.421) | copy-start | bytes 24580
  10.2 546.6 %copy-start.28 = (f32[128,16]{0,1:T(8,128)}, f32[128,16]{0,1:T(8,128)S(1)}, u32[]{:S(2)}) copy-start(f32[128,16]{0,1:T(8,128)S(1)} %get-tuple-element.422) | copy-start | bytes 24580
  10.8 509.0 %copy-start.14 = (f32[2048]{0:T(1024)}, f32[2048]{0:T(1024)S(1)}, u32[]{:S(2)}) copy-start(f32[2048]{0:T(1024)S(1)} %get-tuple-element.416) | copy-start | bytes 24580
  10.8 509.0 %copy-start.16 = (f32[2048]{0:T(1024)}, f32[2048]{0:T(1024)S(1)}, u32[]{:S(2)}) copy-start(f32[2048]{0:T(1024)S(1)} %get-tuple-element.415) | copy-start | bytes 24580
  556.8 332.2 %copy-start.8 = (bf16[1,128,2048]{2,1,0:T(8,128)(2,1)S(1)}, bf16[1,128,2048]{2,1,0:T(8,128)(2,1)}, u32[]{:S(2)}) copy-start(bf16[1,128,2048]{2,1,0:T(8,128)(2,1)} %param.22) | copy-start | bytes 1572868
  559.8 484.3 %all-gather.14.cloned.1.call-start = ((), (), s32[]{:S(2)}) async-start(), calls=%async_computation.8 | async-start | bytes 4718592 | tf_op jit(solution)/shard_map/all_gather | solution.py:209
  560.4 508.3 %all-gather.16.cloned.1.call-start = ((), (), s32[]{:S(2)}) async-start(), calls=%async_computation.9 | async-start | bytes 4718592 | tf_op jit(solution)/shard_map/all_gather | solution.py:210
  913.6 342.5 %reduce-scatter.8.cloned.1.call-start = ((), (), s32[]{:S(2)}) async-start(), calls=%async_computation.10 | async-start | bytes 9437184 | tf_op jit(solution)/shard_map/reduce_scatter | solution.py:260
  1167.6 493.6 %reduce-scatter.16.cloned.1.call-start = ((), (), s32[]{:S(2)}) async-start(), calls=%async_computation.17 | async-start | bytes 47185920
  1193.5 1030.4 %reduce-scatter.10.cloned.1.call-start = ((), (), s32[]{:S(2)}) async-start(), calls=%async_computation.11 | async-start | bytes 66060288 | tf_op jit(solution)/shard_map/reduce_scatter | solution.py:282
  1291.2 995.5 %reduce-scatter.14.cloned.1.call-start = ((), (), s32[]{:S(2)}) async-start(), calls=%async_computation.13 | async-start | bytes 6553600 | tf_op jit(solution)/shard_map/reduce_scatter | solution.py:300
  1661.2 563.5 %copy-start.31 = (f32[3]{0:T(128)S(1)}, f32[3]{0:T(128)}, u32[]{:S(2)}) copy-start(f32[3]{0:T(128)} %param.36) | copy-start | bytes 40
  1661.2 707.1 %reduce-scatter.12.cloned.1.call-start = ((), (), s32[]{:S(2)}) async-start(), calls=%async_computation.12 | async-start | bytes 9175040 | tf_op jit(solution)/shard_map/reduce_scatter | solution.py:299
  2223.9 272.0 %all-reduce.9.cloned.1.call-start = ((), (), s32[]{:S(2)}) async-start(), calls=%async_computation.14 | async-start | bytes 163840 | tf_op jit(solution)/shard_map/psum | solution.py:310
  2258.8 340.2 %all-gather.20.cloned.1.call-start = ((), (), s32[]{:S(2)}) async-start(), calls=%async_computation.16 | async-start | bytes 11796480 | tf_op jit(solution)/shard_map/all_gather | solution.py:323
  2295.1 438.3 %all-gather.18.cloned.1.call-start = ((), (), s32[]{:S(2)}) async-start(), calls=%async_computation.15 | async-start | bytes 16515072 | tf_op jit(solution)/shard_map/all_gather | solution.py:322
  2379.0 116.9 %copy-start.19 = (f32[20480]{0:T(1024)S(1)}, f32[20480]{0:T(1024)}, u32[]{:S(2)}) copy-start(f32[20480]{0:T(1024)} %param.33) | copy-start | bytes 245764
  2379.1 116.9 %copy-start.24 = (f32[20480]{0:T(1024)S(1)}, f32[20480]{0:T(1024)}, u32[]{:S(2)}) copy-start(f32[20480]{0:T(1024)} %param.35) | copy-start | bytes 245764
  (28 other events, 417.0 us)
Sparse Core Ops, SparseCore 0:
  9.9 509.8 all-gather.7
  521.6 367.2 all-gather.11
  891.1 82.0 all-gather.9
  975.2 46.2 all-gather.13
  1023.5 45.0 all-gather.15
  1167.7 88.3 reduce-scatter.7
  1258.4 402.6 reduce-scatter.15
  1663.5 560.2 reduce-scatter.9
  2226.9 59.7 reduce-scatter.13
  2289.5 78.7 reduce-scatter.11
  2374.4 121.4 all-reduce.8
  2497.4 101.4 all-gather.19
  2601.1 132.2 all-gather.17
